TPU v7x, 256 devices: a whole 4x4x8 slice. The times are simulated.
256 devices in a mesh: req: 64 (over y, z_hi, x, core), dec: 4 (over z_lo).
Axes of the slice: x: 4, y: 4, z: 8 (z_hi: 2, z_lo: 4; z = z_hi * 4 + z_lo), core: 2. Of those that a mesh axis runs over, the one named last changes fastest.
Arguments:
- queries: bfloat16 [32768, 2048], P('req', 'dec')
- keys: bfloat16 [32768, 2048], P('req', 'dec'), may hold values from -6 to 6
- values: bfloat16 [32768, 2048], P('req', 'dec'), may hold values from -6 to 6
- resid: bfloat16 [32768, 2048], P('req', 'dec'), may hold values from -6 to 6
- seg_ids: int32 [32768], P('req'), may hold values from -1 to 7, as said below
- out_weight: bfloat16 [2048, 2048], P('dec'), may hold values from -0.125 to 0.125
- norm_gain: float32 [2048], replicated, may hold values from 0.1 to 1.9
- adapter_down: bfloat16 [2048, 128], replicated, may hold values from -0.125 to 0.125
- adapter_up: bfloat16 [128, 4096], P(None, ('req', 'dec')), may hold values from -0.5 to 0.5
- gate_weight: bfloat16 [2048, 4096], P(None, ('req', 'dec')), may hold values from -0.125 to 0.125
- up_weight: bfloat16 [2048, 4096], P(None, ('req', 'dec')), may hold values from -0.125 to 0.125
- down_weight: bfloat16 [4096, 2048], P(('req', 'dec')), may hold values from -0.09375 to 0.09375
- row_order: int32 [64, 512], P('req'), may hold values from 0 to 511, each once within a row
- block_table: int32 [64, 8], P('req'), may hold values from 0 to 7, each once within a row
Outputs:
- block_out: bfloat16 [32768, 2048], P('req', 'dec')
- kv_cache: bfloat16 [512, 64, 4096], P(('req', 'dec'))
Inputs may be any that keep to these rules, and one draw needn't show every extreme that they name: `seg_ids`: within each index of req the live slots come first, grouped into requests whose numbers start at 0, rise by one from request to request and never fall, then come padding slots marked -1; some index of req holds one request that fills all its 512 slots, and when there is more than one index of req, some other index holds request numbers up to the stated most.
All inputs are finite; a program needn't handle non-finite values.
Results may differ from a plain program's by a relative error of at most 0.017.
Values may be sent and summed in bfloat16 or wider, within the bound.
A program may use at most 128 MiB of HBM per device.

v0:
```python
import jax
import jax.numpy as jnp
from jax import lax
from jax.sharding import PartitionSpec as P

HD = 128


def attend(query_rows, key_rows, value_rows, segment):
    row_count = query_rows.shape[0]
    head_count = query_rows.shape[1] // HD
    query_heads = query_rows.reshape(row_count, head_count, HD)
    key_heads = key_rows.reshape(row_count, head_count, HD)
    value_heads = value_rows.reshape(row_count, head_count, HD)
    scores = jnp.einsum(
        "qhd,khd->hqk", query_heads, key_heads, preferred_element_type=jnp.float32
    ) * HD ** (-0.5)
    position = jnp.arange(row_count)
    allowed = (
        (segment[:, None] == segment[None, :])
        & (position[None, :] <= position[:, None])
        & (segment[:, None] >= 0)
    )
    masked = jnp.where(allowed[None], scores, -1e30)
    highest = jnp.max(masked, axis=-1, keepdims=True)
    exponent = jnp.where(allowed[None], jnp.exp(masked - highest), 0.0)
    denominator = jnp.sum(exponent, axis=-1, keepdims=True)
    denominator = jnp.where(denominator > 0, denominator, 1.0)
    weights = (exponent / denominator).astype(jnp.bfloat16)
    result = jnp.einsum("hqk,khd->qhd", weights, value_heads, preferred_element_type=jnp.float32)
    return result.astype(jnp.bfloat16).reshape(row_count, head_count * HD)


def body(
    queries,
    keys,
    values,
    resid,
    seg_ids,
    out_weight,
    norm_gain,
    adapter_down,
    adapter_up,
    gate_weight,
    up_weight,
    down_weight,
    row_order,
    block_table,
):
    slot_count = queries.shape[0]
    features = keys.shape[1]
    block_count = block_table.shape[1]
    block_slots = slot_count // block_count
    table_row = block_table[0]
    placement = (jnp.arange(block_count)[:, None] == table_row[None, :]).astype(jnp.bfloat16)
    key_blocks = keys.reshape(block_count, block_slots, features)
    value_blocks = values.reshape(block_count, block_slots, features)
    ordered_keys = jnp.einsum(
        "tj,jbw->tbw", placement, key_blocks, preferred_element_type=jnp.float32
    ).astype(jnp.bfloat16)
    ordered_values = jnp.einsum(
        "tj,jbw->tbw", placement, value_blocks, preferred_element_type=jnp.float32
    ).astype(jnp.bfloat16)
    moved_keys, moved_values = (
        lax.all_to_all(ordered_keys, "dec", split_axis=0, concat_axis=2, tiled=True),
        lax.all_to_all(ordered_values, "dec", split_axis=0, concat_axis=2, tiled=True),
    )
    kv_cache = jnp.concatenate([moved_keys, moved_values], axis=2)
    attn = attend(queries, keys, values, seg_ids)
    partial_value = jnp.dot(attn, out_weight, preferred_element_type=jnp.float32).astype(
        jnp.bfloat16
    )
    head_total = lax.psum_scatter(partial_value, "dec", scatter_dimension=1, tiled=True).astype(
        jnp.float32
    )
    hidden = (resid.astype(jnp.float32) + head_total).astype(jnp.bfloat16)
    permuted = jnp.take(hidden, row_order[0], axis=0)
    whole_rows = lax.all_gather(permuted, "dec", axis=1, tiled=True)
    mixed_rows = lax.all_to_all(whole_rows, "req", split_axis=0, concat_axis=0, tiled=True)
    quarter = resid.shape[1]
    column = lax.dynamic_slice_in_dim(mixed_rows, lax.axis_index("dec") * quarter, quarter, 1)
    values_f = mixed_rows.astype(jnp.float32)
    scale = lax.rsqrt(jnp.mean(values_f * values_f, axis=-1, keepdims=True) + 1e-05)
    normed = (values_f * scale * norm_gain).astype(jnp.bfloat16)
    low_rank = jnp.dot(normed, adapter_down, preferred_element_type=jnp.float32).astype(
        jnp.bfloat16
    )
    operand = jnp.concatenate([normed, low_rank], axis=1)
    rank_width = adapter_down.shape[1]
    piece_width = gate_weight.shape[1]
    padding = jnp.zeros((rank_width, piece_width), jnp.bfloat16)
    stacked = jnp.stack(
        [
            jnp.concatenate([gate_weight, adapter_up], axis=0),
            jnp.concatenate([up_weight, padding], axis=0),
        ]
    )
    projected = jnp.einsum(
        "md,gdc->gmc",
        operand,
        lax.all_gather(stacked, "req", axis=2, tiled=True),
        preferred_element_type=jnp.float32,
    )
    hidden_units = (jax.nn.gelu(projected[0]) * projected[1]).astype(jnp.bfloat16)
    down_full = lax.all_gather(down_weight, "req", axis=0, tiled=True)
    down_part = jnp.dot(hidden_units, down_full, preferred_element_type=jnp.float32).astype(
        jnp.bfloat16
    )
    mlp_total = lax.psum_scatter(down_part, "dec", scatter_dimension=1, tiled=True).astype(
        jnp.float32
    )
    block_out = (column.astype(jnp.float32) + mlp_total).astype(jnp.bfloat16)
    return (block_out, kv_cache)


def solution(mesh):
    placed = (
        P("req", "dec"),
        P("req", "dec"),
        P("req", "dec"),
        P("req", "dec"),
        P("req"),
        P("dec", None),
        P(),
        P(),
        P(None, ("req", "dec")),
        P(None, ("req", "dec")),
        P(None, ("req", "dec")),
        P(("req", "dec"), None),
        P("req", None),
        P("req", None),
    )
    return jax.shard_map(
        body,
        mesh=mesh,
        in_specs=placed,
        out_specs=(P("req", "dec"), P(("req", "dec"), None, None)),
        check_vma=False,
    )
```

profile of v0, /device:TPU:1, one launch (start us, length us, event | category | flops | bytes accessed | tf_op | source)
XLA Modules:
  0.0 435.6 jit_solution(6591187465169870902)
XLA Ops:
  7.2 0.0 copy-start
  7.2 0.0 reduce-scatter.3.cloned.1.call-start
  7.2 0.8 broadcast_compare_fusion
  8.1 1.0 fusion.26
  9.0 1.9 fusion.27
  10.9 0.0 copy-start.4
  11.0 4.1 fusion.46
  15.1 0.0 copy-done.4
  15.1 0.2 copy.44
  15.3 2.6 fusion.19
  18.0 0.0 copy-start.11
  18.0 0.0 copy-start.6
  18.0 0.0 copy-done
  18.0 2.6 convolution_convert_fusion.1
  20.6 0.0 reduce-scatter.3.cloned.1.call-update
  20.6 0.0 copy-start.8
  20.6 0.0 copy-start.9
  20.7 0.0 copy-start.12
  20.7 0.0 all-gather.4.cloned.1.call-start
  20.7 0.0 copy-done.11
  20.8 52.3 %reduce-scatter.3.cloned.1.call-done = bf16[512,512]{1,0:T(8,128)(2,1)} async-done(((bf16[512,2048]{1,0:T(8,128)(2,1)}), bf16[512,512]{1,0:T(8,128)(2,1)}) %reduce-scatter.3.cloned.1.call-update) | async-done | bytes 524304 | tf_op jit(solution)/shard_map/reduce_scatter | solution.py:73
  73.1 0.0 copy-done.6
  73.1 1.2 add_convert_fusion.1
  74.3 2.0 gather_fusion
  76.2 0.0 copy-start.10
  76.2 0.9 broadcast_select_fusion
  77.2 0.0 all-gather.4.cloned.1.call-update
  77.2 0.0 all-gather.6.cloned.1.call-start
  77.2 0.0 copy-done.8
  77.3 0.0 copy-done.9
  77.3 0.0 copy-done.12
  77.3 0.7 pad_maximum_fusion.1
  78.0 0.0 all-gather.6.cloned.1.call-update
  78.0 0.0 all-gather.8.cloned.1.call-start
  78.1 0.5 all-gather.8.cloned.1.call-update
  78.6 0.0 reduce-scatter.5.cloned.1.call-start
  78.6 48.0 %all-gather.4.cloned.1.call-done = bf16[512,2048]{1,0:T(8,128)(2,1)} async-done(((bf16[512,512]{1,0:T(8,128)(2,1)}), bf16[512,2048]{1,0:T(8,128)(2,1)}) %all-gather.4.cloned.1.call-update) | async-done | bytes 2097168 | tf_op jit(solution)/shard_map/all_gather | solution.py:78
  126.7 62.3 %all_to_all.48 = bf16[64,8,2048]{2,1,0:T(8,128)(2,1)S(1)} all-to-all(bf16[64,8,2048]{2,1,0:T(8,128)(2,1)} %bitcast.72), channel_id=1, replica_groups=mesh['req'=64,'dec'=4] {'req'}, dimensions={0} | all-to-all | bytes 4194304 | tf_op jit(solution)/shard_map/all_to_all | solution.py:79
  188.9 1.3 copy-done.1
  190.3 0.5 multiply_reduce_fusion
  190.8 0.1 rsqrt.12
  190.9 0.0 copy-done.10
  190.9 2.1 multiply_convert_fusion
  193.0 0.0 copy-start.2
  193.0 1.3 copy-done.2
  194.3 0.8 convolution_convert_fusion.4
  195.2 0.1 copy.36
  195.3 70.0 %all-gather.6.cloned.1.call-done = bf16[2,2176,1024]{1,2,0:T(8,128)(2,1)} async-done(((bf16[2,2176,16]{1,2,0:T(8,128)(2,1)}), bf16[2,2176,1024]{1,2,0:T(8,128)(2,1)}) %all-gather.6.cloned.1.call-update) | async-done | bytes 8912912 | tf_op jit(solution)/shard_map/all_gather | solution.py:101
  265.3 10.6 %fusion.5 = f32[2,512,1024]{1,2,0:T(8,128)} fusion(bf16[2,2176,1024]{1,2,0:T(8,128)(2,1)} %all-gather.6.cloned.1.call-done, bf16[512,128]{1,0:T(8,128)(2,1)S(1)} %copy.36, bf16[512,2048]{1,0:T(8,128)(2,1)} %copy-done.2), kind=kOutput, calls=%fused_computation.15 | convolution fusion | flops 4567859200 | bytes 15335424 | tf_op jit(solution)/shard_map/md,gdc->gmc/dot_general | solution.py:98
  275.9 79.1 %all-gather.8.cloned.1.call-done = bf16[1024,2048]{1,0:T(8,128)(2,1)} async-done(((bf16[16,2048]{1,0:T(8,128)(2,1)}), bf16[1024,2048]{1,0:T(8,128)(2,1)}) %all-gather.8.cloned.1.call-update) | async-done | bytes 4194320 | tf_op jit(solution)/shard_map/all_gather | solution.py:105
  355.0 7.4 %convolution_convert_fusion = bf16[512,2048]{1,0:T(8,128)(2,1)} fusion(bf16[1024,2048]{1,0:T(8,128)(2,1)} %all-gather.8.cloned.1.call-done, f32[2,512,1024]{1,2,0:T(8,128)} %fusion.5), kind=kOutput, calls=%fused_computation.9 | convolution fusion | flops 2153775104 | bytes 10485760 | tf_op jit(solution)/shard_map/dot_general | solution.py:106
  362.3 0.0 reduce-scatter.5.cloned.1.call-update
  362.4 0.4 convolution_convert_fusion.3
  362.8 0.9 copy.38
  363.7 3.5 all-to-all-start.1
  367.2 0.0 copy-done.5
  367.2 0.4 convolution_convert_fusion.2
  367.6 0.9 copy.41
  368.6 27.2 %all-to-all-done.1 = bf16[8,64,512]{2,1,0:T(8,128)(2,1)S(1)} async-done(((bf16[8,64,512]{2,1,0:T(8,128)(2,1)}), bf16[8,64,512]{2,1,0:T(8,128)(2,1)S(1)}, u32[]{:S(2)}, u32[]{:S(2)}) %all-to-all-start.1) | async-done | bytes 524320 | tf_op jit(solution)/shard_map/all_to_all | solution.py:65
  395.8 3.5 all-to-all-start.2
  399.3 0.9 copy.47
  400.2 24.6 %all-to-all-done.2 = bf16[8,64,512]{2,1,0:T(8,128)(2,1)S(1)} async-done(((bf16[8,64,512]{2,1,0:T(8,128)(2,1)}), bf16[8,64,512]{2,1,0:T(8,128)(2,1)S(1)}, u32[]{:S(2)}, u32[]{:S(2)}) %all-to-all-start.2) | async-done | bytes 524320 | tf_op jit(solution)/shard_map/all_to_all | solution.py:66
  424.8 2.1 pad_maximum_fusion
  426.9 2.1 add_convert_fusion
  (16 shorter events, 0.1 us)
Async XLA Ops:
  7.2 10.8 %copy-start = (bf16[512,2048]{1,0:T(8,128)(2,1)S(1)}, bf16[512,2048]{1,0:T(8,128)(2,1)}, u32[]{:S(2)}) copy-start(bf16[512,2048]{1,0:T(8,128)(2,1)} %param.19) | copy-start | bytes 6291460
  7.2 65.9 %reduce-scatter.3.cloned.1.call-start = ((), (), s32[]{:S(2)}) async-start(), calls=%async_computation.5 | async-start | bytes 2621440 | tf_op jit(solution)/shard_map/reduce_scatter | solution.py:73
  10.9 4.1 copy-start.4
  18.0 2.8 copy-start.11
  18.0 55.1 %copy-start.6 = (bf16[512,512]{1,0:T(8,128)(2,1)S(1)}, bf16[512,512]{1,0:T(8,128)(2,1)}, u32[]{:S(2)}) copy-start(bf16[512,512]{1,0:T(8,128)(2,1)} %param.17) | copy-start | bytes 1572868
  20.6 56.6 %copy-start.8 = (bf16[2048,16]{0,1:T(8,128)(2,1)S(1)}, bf16[2048,16]{0,1:T(8,128)(2,1)}, u32[]{:S(2)}) copy-start(bf16[2048,16]{0,1:T(8,128)(2,1)} %param.23) | copy-start | bytes 196612
  20.6 56.6 %copy-start.9 = (bf16[2048,16]{0,1:T(8,128)(2,1)S(1)}, bf16[2048,16]{0,1:T(8,128)(2,1)}, u32[]{:S(2)}) copy-start(bf16[2048,16]{0,1:T(8,128)(2,1)} %param.24) | copy-start | bytes 196612
  20.7 56.6 %copy-start.12 = (bf16[128,16]{0,1:T(8,128)(2,1)S(1)}, bf16[128,16]{0,1:T(8,128)(2,1)}, u32[]{:S(2)}) copy-start(bf16[128,16]{0,1:T(8,128)(2,1)} %param.22) | copy-start | bytes 12292
  20.7 106.0 %all-gather.4.cloned.1.call-start = ((), (), s32[]{:S(2)}) async-start(), calls=%async_computation.6 | async-start | bytes 2621440 | tf_op jit(solution)/shard_map/all_gather | solution.py:78
  76.2 114.6 %copy-start.10 = (f32[2048]{0:T(1024)S(1)}, f32[2048]{0:T(1024)}, u32[]{:S(2)}) copy-start(f32[2048]{0:T(1024)} %param.20) | copy-start | bytes 24580
  77.2 188.1 %all-gather.6.cloned.1.call-start = ((), (), s32[]{:S(2)}) async-start(), calls=%async_computation.7 | async-start | bytes 9052160 | tf_op jit(solution)/shard_map/all_gather | solution.py:101
  78.0 277.0 %all-gather.8.cloned.1.call-start = ((), (), s32[]{:S(2)}) async-start(), calls=%async_computation.8 | async-start | bytes 4259840 | tf_op jit(solution)/shard_map/all_gather | solution.py:105
  78.6 348.3 %reduce-scatter.5.cloned.1.call-start = ((), (), s32[]{:S(2)}) async-start(), calls=%async_computation.9 | async-start | bytes 2621440 | tf_op jit(solution)/shard_map/reduce_scatter | solution.py:109
  188.9 1.3 copy-start.1
  190.3 4.1 copy-start.7
  193.0 1.3 copy-start.2
  275.9 86.5 %copy-start.3 = (bf16[512,512]{1,0:T(8,128)(2,1)S(1)}, bf16[512,512]{1,0:T(8,128)(2,1)}, u32[]{:S(2)}) copy-start(bf16[512,512]{1,0:T(8,128)(2,1)} %param.15) | copy-start | bytes 1572868
  275.9 86.5 %copy-start.13 = (s32[1,8]{1,0:T(1,128)S(1)}, s32[1,8]{1,0:T(1,128)}, u32[]{:S(2)}) copy-start(s32[1,8]{1,0:T(1,128)} %param.27) | copy-start | bytes 100
  362.3 4.9 %copy-start.5 = (bf16[512,512]{1,0:T(8,128)(2,1)S(1)}, bf16[512,512]{1,0:T(8,128)(2,1)}, u32[]{:S(2)}) copy-start(bf16[512,512]{1,0:T(8,128)(2,1)} %param.16) | copy-start | bytes 1572868
  363.7 32.1 %all-to-all-start.1 = ((bf16[8,64,512]{2,1,0:T(8,128)(2,1)}), bf16[8,64,512]{2,1,0:T(8,128)(2,1)S(1)}, u32[]{:S(2)}, u32[]{:S(2)}) async-start(bf16[8,64,512]{2,1,0:T(8,128)(2,1)} %copy.38), calls=%async_computation.3 | async-start | bytes 1048576 | tf_op jit(solution)/shard_map/all_to_all | solution.py:65
  395.8 28.9 %all-to-all-start.2 = ((bf16[8,64,512]{2,1,0:T(8,128)(2,1)}), bf16[8,64,512]{2,1,0:T(8,128)(2,1)S(1)}, u32[]{:S(2)}, u32[]{:S(2)}) async-start(bf16[8,64,512]{2,1,0:T(8,128)(2,1)} %copy.41), calls=%async_computation.4 | async-start | bytes 1048576 | tf_op jit(solution)/shard_map/all_to_all | solution.py:66
Sparse Core Ops, SparseCore 0:
  20.8 52.2 reduce-scatter.2
  77.3 49.2 all-gather.3
  131.0 134.2 all-gather.5
  268.7 86.1 all-gather.7
  362.5 57.5 reduce-scatter.4
where the time goes:
time: 436 us
  waiting for transfers between devices  302 us (69%)
  blocking collectives  62.3 us (14%)
  matrix products  26.7 us (6%)
  other arithmetic  15.6 us (4%)
  between operations  14.1 us (3%)
  local copies, waits for them, and re-layouts  7.92 us (2%)
  starting transfers between devices  7.15 us (2%)
    all_gather x1, waiting for transfers between devices, body(): down_full = lax.all_gather(down_weight, 'req', axis=0, tiled=True)  79.1 us
    all_gather x1, waiting for transfers between devices, body(): lax.all_gather(stacked, 'req', axis=2, tiled=True)  70 us
    all_to_all x1, blocking collectives, body(): lax.all_to_all(whole_rows, 'req', split_axis=0, concat_axis=0, tiled=True)  62.3 us
    reduce_scatter x1, waiting for transfers between devices, body(): lax.psum_scatter(partial_value, 'dec', scatter_dimension=1, tiled=True)  52.3 us
    all_gather x1, waiting for transfers between devices, body(): whole_rows = lax.all_gather(permuted, 'dec', axis=1, tiled=True)  48 us
    all_to_all x1, waiting for transfers between devices, body(): lax.all_to_all(ordered_keys, 'dec', split_axis=0, concat_axis=2, tiled=True)  27.2 us
    all_to_all x1, waiting for transfers between devices, body(): lax.all_to_all(ordered_values, 'dec', split_axis=0, concat_axis=2, tiled=...  24.6 us
    dot_general x1, matrix products, body(): jnp.einsum('md,gdc->gmc', operand, lax.all_gather(stacked, 'req', axis=2,...  10.6 us
  transfers between devices with their start and end apart: 7, of which 6 were waited for; matrix products, arithmetic and copies ran while one was open for 5% of the time, Pallas kernels for 0%

commit v1 on v0

--- a/solution.py
+++ b/solution.py
@@ -2,6 +2,7 @@
 import jax.numpy as jnp
 from jax import lax
 from jax.sharding import PartitionSpec as P
+from jax.lax import all_to_all, axis_size
 
 HD = 128
 
@@ -95,11 +96,21 @@
             jnp.concatenate([up_weight, padding], axis=0),
         ]
     )
+
+    def _use_tracks(in_array, out_dim):
+        f_next = jnp.concatenate(
+            all_to_all(
+                jnp.stack([in_array] * axis_size("req"), 0),
+                axis_name="req",
+                split_axis=0,
+                concat_axis=0,
+            ),
+            out_dim,
+        )
+        return f_next
+
     projected = jnp.einsum(
-        "md,gdc->gmc",
-        operand,
-        lax.all_gather(stacked, "req", axis=2, tiled=True),
-        preferred_element_type=jnp.float32,
+        "md,gdc->gmc", operand, _use_tracks(stacked, 2), preferred_element_type=jnp.float32
     )
     hidden_units = (jax.nn.gelu(projected[0]) * projected[1]).astype(jnp.bfloat16)
     down_full = lax.all_gather(down_weight, "req", axis=0, tiled=True)

time: 436 us -> 538 us (1.23)
  waiting for transfers between devices: 302 us -> 437 us
  blocking collectives: 62.3 us -> 0 us
  starting transfers between devices: 7.15 us -> 26.7 us
  local copies, waits for them, and re-layouts: 7.92 us -> 18.6 us
    all_to_all x0 -> x2, waiting for transfers between devices: none -> 151 us  [the longest x1 102 us: _use_tracks(): all_to_all(jnp.stack([in_array] * axis_size('req'), 0), axis_name='req',...]
    all_gather x1 -> x0, waiting for transfers between devices: 70 us -> none  [body(): lax.all_gather(stacked, 'req', axis=2, tiled=True)]
    all_to_all x1 -> x0, blocking collectives: 62.3 us -> none  [body(): lax.all_to_all(whole_rows, 'req', split_axis=0, concat_axis=0, tiled=True)]
    all_gather x1, waiting for transfers between devices: 79.1 us -> 132 us  [body(): down_full = lax.all_gather(down_weight, 'req', axis=0, tiled=True)]
    all_to_all x0 -> x2, starting transfers between devices: none -> 19.4 us  [the longest x1 11.9 us: body(): lax.all_to_all(whole_rows, 'req', split_axis=0, concat_axis=0, tiled=True)]
    reshape x0 -> x1, local copies, waits for them, and re-layouts: none -> 7.79 us  [_use_tracks(): jnp.concatenate(all_to_all(jnp.stack([in_array] * axis_size('req'), 0), a...]
  transfers between devices with their start and end apart: 7 -> 8, of which waited for: 6 -> 7; matrix products, arithmetic and copies ran while one was open for 5% -> 5% of each run, Pallas kernels for 0% -> 0%
where the time goes in v1:
time: 538 us
  waiting for transfers between devices  437 us (81%)
  starting transfers between devices  26.7 us (5%)
  matrix products  26.5 us (5%)
  local copies, waits for them, and re-layouts  18.6 us (3%)
  between operations  15.5 us (3%)
  other arithmetic  13.4 us (2%)
    all_gather x1, waiting for transfers between devices, body(): down_full = lax.all_gather(down_weight, 'req', axis=0, tiled=True)  132 us
    all_to_all x1, waiting for transfers between devices, _use_tracks(): all_to_all(jnp.stack([in_array] * axis_size('req'), 0), axis_name='req',...  102 us
    reduce_scatter x1, waiting for transfers between devices, body(): lax.psum_scatter(partial_value, 'dec', scatter_dimension=1, tiled=True)  52.3 us
    all_gather x1, waiting for transfers between devices, body(): whole_rows = lax.all_gather(permuted, 'dec', axis=1, tiled=True)  49.5 us
    all_to_all x1, waiting for transfers between devices, body(): lax.all_to_all(whole_rows, 'req', split_axis=0, concat_axis=0, tiled=True)  49.4 us
    all_to_all x1, waiting for transfers between devices, body(): lax.all_to_all(ordered_keys, 'dec', split_axis=0, concat_axis=2, tiled=True)  27.2 us
    all_to_all x1, waiting for transfers between devices, body(): lax.all_to_all(ordered_values, 'dec', split_axis=0, concat_axis=2, tiled=...  24.6 us
    all_to_all x1, starting transfers between devices, body(): lax.all_to_all(whole_rows, 'req', split_axis=0, concat_axis=0, tiled=True)  11.9 us
  transfers between devices with their start and end apart: 8, of which 7 were waited for; matrix products, arithmetic and copies ran while one was open for 5% of the time, Pallas kernels for 0%

profile of v1, /device:TPU:1, one launch (start us, length us, event | category | flops | bytes accessed | tf_op | source)
XLA Modules:
  0.0 537.8 jit_solution(3814338849770487057)
XLA Ops:
  8.0 0.0 copy-start
  8.0 0.0 reduce-scatter.3.cloned.1.call-start
  8.1 0.8 broadcast_compare_fusion
  8.9 1.0 fusion.26
  9.9 1.9 fusion.27
  11.8 0.0 copy-start.6
  11.8 4.1 fusion.46
  15.9 0.0 copy-done.6
  15.9 0.2 copy.45
  16.1 2.6 fusion.19
  18.8 0.0 copy-start.12
  18.8 0.0 copy-start.7
  18.8 0.0 copy-done
  18.8 2.6 convolution_convert_fusion.1
  21.4 0.0 reduce-scatter.3.cloned.1.call-update
  21.5 0.0 all-gather.3.cloned.1.call-start
  21.5 0.0 copy-done.12
  21.6 52.3 %reduce-scatter.3.cloned.1.call-done = bf16[512,512]{1,0:T(8,128)(2,1)} async-done(((bf16[512,2048]{1,0:T(8,128)(2,1)}), bf16[512,512]{1,0:T(8,128)(2,1)}) %reduce-scatter.3.cloned.1.call-update) | async-done | bytes 524304 | tf_op jit(solution)/shard_map/reduce_scatter | solution.py:74
  73.9 0.0 copy-done.7
  73.9 1.2 add_convert_fusion.1
  75.1 0.0 copy-start.9
  75.1 0.0 copy-start.10
  75.1 0.0 copy-start.13
  75.1 2.0 gather_fusion
  77.1 0.9 broadcast_select_fusion
  78.0 0.0 all-gather.3.cloned.1.call-update
  78.0 49.5 %all-gather.3.cloned.1.call-done = bf16[512,2048]{1,0:T(8,128)(2,1)} async-done(((bf16[512,512]{1,0:T(8,128)(2,1)}), bf16[512,2048]{1,0:T(8,128)(2,1)}) %all-gather.3.cloned.1.call-update) | async-done | bytes 2097168 | tf_op jit(solution)/shard_map/all_gather | solution.py:79
  127.5 11.9 %all-to-all-start = ((bf16[64,8,2048]{2,1,0:T(8,128)(2,1)}), bf16[64,8,2048]{2,1,0:T(8,128)(2,1)S(1)}, u32[]{:S(2)}, u32[]{:S(2)}) async-start(bf16[64,8,2048]{2,1,0:T(8,128)(2,1)} %bitcast.75), calls=%async_computation.1 | async-start | bytes 4194304 | tf_op jit(solution)/shard_map/all_to_all | solution.py:80
  139.4 0.0 copy-done.9
  139.5 49.4 %all-to-all-done = bf16[64,8,2048]{2,1,0:T(8,128)(2,1)S(1)} async-done(((bf16[64,8,2048]{2,1,0:T(8,128)(2,1)}), bf16[64,8,2048]{2,1,0:T(8,128)(2,1)S(1)}, u32[]{:S(2)}, u32[]{:S(2)}) %all-to-all-start) | async-done | bytes 2097184 | tf_op jit(solution)/shard_map/all_to_all | solution.py:80
  188.9 4.1 stack.11
  193.0 7.5 %all-to-all-start.1 = ((bf16[64,2,2176,16]{2,3,1,0:T(8,128)(2,1)}), bf16[64,2,2176,16]{2,3,1,0:T(8,128)(2,1)}, u32[]{:S(2)}, u32[]{:S(2)}) async-start(bf16[64,2,2176,16]{2,3,1,0:T(8,128)(2,1)} %stack.11), calls=%async_computation.2 | async-start | bytes 17825792 | tf_op jit(solution)/shard_map/all_to_all | solution.py:102
  200.5 0.0 copy-start.8
  200.5 0.0 all-gather.5.cloned.1.call-start
  200.6 0.5 all-gather.5.cloned.1.call-update
  201.1 0.2 reduce-scatter.5.cloned.1.call-start
  201.3 0.5 multiply_reduce_fusion
  201.8 0.1 rsqrt.12
  201.9 0.0 copy-done.11
  202.0 0.5 multiply_convert_fusion
  202.5 0.0 copy-start.3
  202.5 1.4 copy-done.3
  203.9 0.8 convolution_convert_fusion.4
  204.8 0.1 copy.37
  204.9 102.0 %all-to-all-done.1 = bf16[64,2,2176,16]{2,3,1,0:T(8,128)(2,1)} async-done(((bf16[64,2,2176,16]{2,3,1,0:T(8,128)(2,1)}), bf16[64,2,2176,16]{2,3,1,0:T(8,128)(2,1)}, u32[]{:S(2)}, u32[]{:S(2)}) %all-to-all-start.1) | async-done | bytes 8912928 | tf_op jit(solution)/shard_map/all_to_all | solution.py:102
  306.9 7.8 %copy.36 = bf16[2,2176,64,16]{1,3,2,0:T(8,128)(2,1)} copy(bf16[2,2176,64,16]{1,3,0,2:T(8,128)(2,1)} %bitcast.10) | data formatting | bytes 17825792 | tf_op jit(solution)/shard_map/reshape | solution.py:101
  314.7 10.3 %fusion.5 = f32[2,512,1024]{1,2,0:T(8,128)} fusion(bf16[2,2176,1024]{1,2,0:T(8,128)(2,1)} %bitcast.73, bf16[512,128]{1,0:T(8,128)(2,1)S(1)} %copy.37, bf16[512,2048]{1,0:T(8,128)(2,1)S(1)} %copy-done.4), kind=kOutput, calls=%fused_computation.15 | convolution fusion | flops 4567859200 | bytes 15335424 | tf_op jit(solution)/shard_map/md,gdc->gmc/dot_general | solution.py:112
  325.0 131.6 %all-gather.5.cloned.1.call-done = bf16[1024,2048]{1,0:T(8,128)(2,1)} async-done(((bf16[16,2048]{1,0:T(8,128)(2,1)}), bf16[1024,2048]{1,0:T(8,128)(2,1)}) %all-gather.5.cloned.1.call-update) | async-done | bytes 4194320 | tf_op jit(solution)/shard_map/all_gather | solution.py:116
  456.6 7.4 %convolution_convert_fusion = bf16[512,2048]{1,0:T(8,128)(2,1)} fusion(bf16[1024,2048]{1,0:T(8,128)(2,1)} %all-gather.5.cloned.1.call-done, f32[2,512,1024]{1,2,0:T(8,128)} %fusion.5), kind=kOutput, calls=%fused_computation.9 | convolution fusion | flops 2153775104 | bytes 10485760 | tf_op jit(solution)/shard_map/dot_general | solution.py:117
  464.0 0.0 reduce-scatter.5.cloned.1.call-update
  464.0 0.0 copy-done.5
  464.0 0.0 copy-done.14
  464.0 0.4 convolution_convert_fusion.3
  464.4 0.9 copy.39
  465.4 3.5 all-to-all-start.2
  468.9 0.0 copy-start.1
  468.9 0.4 convolution_convert_fusion.2
  469.3 0.9 copy.42
  470.2 27.2 %all-to-all-done.2 = bf16[8,64,512]{2,1,0:T(8,128)(2,1)S(1)} async-done(((bf16[8,64,512]{2,1,0:T(8,128)(2,1)}), bf16[8,64,512]{2,1,0:T(8,128)(2,1)S(1)}, u32[]{:S(2)}, u32[]{:S(2)}) %all-to-all-start.2) | async-done | bytes 524320 | tf_op jit(solution)/shard_map/all_to_all | solution.py:66
  497.5 3.5 all-to-all-start.3
  501.0 0.9 copy.48
  501.8 24.6 %all-to-all-done.3 = bf16[8,64,512]{2,1,0:T(8,128)(2,1)S(1)} async-done(((bf16[8,64,512]{2,1,0:T(8,128)(2,1)}), bf16[8,64,512]{2,1,0:T(8,128)(2,1)S(1)}, u32[]{:S(2)}, u32[]{:S(2)}) %all-to-all-start.3) | async-done | bytes 524320 | tf_op jit(solution)/shard_map/all_to_all | solution.py:67
  526.5 2.1 pad_maximum_fusion
  528.6 2.1 add_convert_fusion
  (20 shorter events, 0.1 us)
Async XLA Ops:
  8.0 10.8 %copy-start = (bf16[512,2048]{1,0:T(8,128)(2,1)S(1)}, bf16[512,2048]{1,0:T(8,128)(2,1)}, u32[]{:S(2)}) copy-start(bf16[512,2048]{1,0:T(8,128)(2,1)} %param.19) | copy-start | bytes 6291460
  8.0 65.9 %reduce-scatter.3.cloned.1.call-start = ((), (), s32[]{:S(2)}) async-start(), calls=%async_computation.6 | async-start | bytes 2621440 | tf_op jit(solution)/shard_map/reduce_scatter | solution.py:74
  11.8 4.1 copy-start.6
  18.8 2.7 copy-start.12
  18.8 55.1 %copy-start.7 = (bf16[512,512]{1,0:T(8,128)(2,1)S(1)}, bf16[512,512]{1,0:T(8,128)(2,1)}, u32[]{:S(2)}) copy-start(bf16[512,512]{1,0:T(8,128)(2,1)} %param.17) | copy-start | bytes 1572868
  21.5 106.1 %all-gather.3.cloned.1.call-start = ((), (), s32[]{:S(2)}) async-start(), calls=%async_computation.7 | async-start | bytes 2621440 | tf_op jit(solution)/shard_map/all_gather | solution.py:79
  75.1 64.4 %copy-start.9 = (bf16[2048,16]{0,1:T(8,128)(2,1)S(1)}, bf16[2048,16]{0,1:T(8,128)(2,1)}, u32[]{:S(2)}) copy-start(bf16[2048,16]{0,1:T(8,128)(2,1)} %param.23) | copy-start | bytes 196612
  75.1 64.4 %copy-start.10 = (bf16[2048,16]{0,1:T(8,128)(2,1)S(1)}, bf16[2048,16]{0,1:T(8,128)(2,1)}, u32[]{:S(2)}) copy-start(bf16[2048,16]{0,1:T(8,128)(2,1)} %param.24) | copy-start | bytes 196612
  75.1 64.4 %copy-start.13 = (bf16[128,16]{0,1:T(8,128)(2,1)S(1)}, bf16[128,16]{0,1:T(8,128)(2,1)}, u32[]{:S(2)}) copy-start(bf16[128,16]{0,1:T(8,128)(2,1)} %param.22) | copy-start | bytes 12292
  127.5 61.4 %all-to-all-start = ((bf16[64,8,2048]{2,1,0:T(8,128)(2,1)}), bf16[64,8,2048]{2,1,0:T(8,128)(2,1)S(1)}, u32[]{:S(2)}, u32[]{:S(2)}) async-start(bf16[64,8,2048]{2,1,0:T(8,128)(2,1)} %bitcast.75), calls=%async_computation.1 | async-start | bytes 4194304 | tf_op jit(solution)/shard_map/all_to_all | solution.py:80
  188.9 13.0 %copy-start.2 = (bf16[64,8,2048]{2,1,0:T(8,128)(2,1)}, bf16[64,8,2048]{2,1,0:T(8,128)(2,1)S(1)}, u32[]{:S(2)}) copy-start(bf16[64,8,2048]{2,1,0:T(8,128)(2,1)S(1)} %all-to-all-done) | copy-start | bytes 6291460
  193.0 8.9 %copy-start.11 = (f32[2048]{0:T(1024)S(1)}, f32[2048]{0:T(1024)}, u32[]{:S(2)}) copy-start(f32[2048]{0:T(1024)} %param.20) | copy-start | bytes 24580
  193.0 113.8 %all-to-all-start.1 = ((bf16[64,2,2176,16]{2,3,1,0:T(8,128)(2,1)}), bf16[64,2,2176,16]{2,3,1,0:T(8,128)(2,1)}, u32[]{:S(2)}, u32[]{:S(2)}) async-start(bf16[64,2,2176,16]{2,3,1,0:T(8,128)(2,1)} %stack.11), calls=%async_computation.2 | async-start | bytes 17825792 | tf_op jit(solution)/shard_map/all_to_all | solution.py:102
  200.5 3.4 copy-start.8
  200.5 256.1 %all-gather.5.cloned.1.call-start = ((), (), s32[]{:S(2)}) async-start(), calls=%async_computation.8 | async-start | bytes 4259840 | tf_op jit(solution)/shard_map/all_gather | solution.py:116
  201.1 327.5 %reduce-scatter.5.cloned.1.call-start = ((), (), s32[]{:S(2)}) async-start(), calls=%async_computation.9 | async-start | bytes 2621440 | tf_op jit(solution)/shard_map/reduce_scatter | solution.py:120
  202.5 1.4 copy-start.3
  306.9 7.8 %copy-start.4 = (bf16[512,2048]{1,0:T(8,128)(2,1)S(1)}, bf16[512,2048]{1,0:T(8,128)(2,1)}, u32[]{:S(2)}) copy-start(bf16[512,2048]{1,0:T(8,128)(2,1)} %copy-done.3) | copy-start | bytes 6291460
  325.0 139.0 %copy-start.5 = (bf16[512,512]{1,0:T(8,128)(2,1)S(1)}, bf16[512,512]{1,0:T(8,128)(2,1)}, u32[]{:S(2)}) copy-start(bf16[512,512]{1,0:T(8,128)(2,1)} %param.15) | copy-start | bytes 1572868
  325.0 139.1 %copy-start.14 = (s32[1,8]{1,0:T(1,128)S(1)}, s32[1,8]{1,0:T(1,128)}, u32[]{:S(2)}) copy-start(s32[1,8]{1,0:T(1,128)} %param.27) | copy-start | bytes 100
  465.4 32.1 %all-to-all-start.2 = ((bf16[8,64,512]{2,1,0:T(8,128)(2,1)}), bf16[8,64,512]{2,1,0:T(8,128)(2,1)S(1)}, u32[]{:S(2)}, u32[]{:S(2)}) async-start(bf16[8,64,512]{2,1,0:T(8,128)(2,1)} %copy.39), calls=%async_computation.4 | async-start | bytes 1048576 | tf_op jit(solution)/shard_map/all_to_all | solution.py:66
  468.9 61.8 %copy-start.1 = (bf16[512,2048]{1,0:T(8,128)(2,1)S(1)}, bf16[512,2048]{1,0:T(8,128)(2,1)}, u32[]{:S(2)}) copy-start(bf16[512,2048]{1,0:T(8,128)(2,1)} %param.19) | copy-start | bytes 6291460
  497.5 28.9 %all-to-all-start.3 = ((bf16[8,64,512]{2,1,0:T(8,128)(2,1)}), bf16[8,64,512]{2,1,0:T(8,128)(2,1)S(1)}, u32[]{:S(2)}, u32[]{:S(2)}) async-start(bf16[8,64,512]{2,1,0:T(8,128)(2,1)} %copy.42), calls=%async_computation.5 | async-start | bytes 1048576 | tf_op jit(solution)/shard_map/all_to_all | solution.py:67
Sparse Core Ops, SparseCore 0:
  21.6 52.2 reduce-scatter.2
  78.2 49.2 all-gather.2
  464.1 57.5 reduce-scatter.4
Sparse Core Ops, SparseCore 1:
  204.6 251.9 all-gather.4
